TPU v7x, 256 devices: a whole 4x4x8 slice. The times are simulated.
256 devices in a mesh: section: 16 (over z_lo, y), dp: 16 (over x, z_hi, core).
Axes of the slice: x: 4, y: 4, z: 8 (z_hi: 2, z_lo: 4; z = z_hi * 4 + z_lo), core: 2. Of those that a mesh axis runs over, the one named last changes fastest.
Arguments:
- enc_state: bfloat16 [16, 512, 4096], P('section', 'dp'), may hold values from -1000 to 1000
- final_gain: float32 [4096], replicated, may hold values from 0.5 to 1.5
- queries: bfloat16 [16, 2048, 4096], P('section', 'dp'), may hold values from -60 to 60
- w_key: bfloat16 [16, 4096, 4096], P('section', None, 'dp'), may hold values from -0.09375 to 0.09375
- w_value: bfloat16 [16, 4096, 4096], P('section', None, 'dp'), may hold values from -0.09375 to 0.09375
- ctx_grad: bfloat16 [16, 2048, 4096], P('section', 'dp'), may hold values from -6 to 6
- mem_len: int32 [16], P('dp'), may hold values from 8 to 32, as said below
Outputs:
- query_grad: bfloat16 [16, 2048, 4096], P('section', 'dp')
- key_weight_grad: bfloat16 [16, 4096, 4096], P('section', None, 'dp')
- value_weight_grad: bfloat16 [16, 4096, 4096], P('section', None, 'dp')
- state_grad: bfloat16 [16, 512, 4096], P('section', 'dp')
- gain_grad: float32 [4096], replicated
Inputs may be any that keep to these rules, and one draw needn't show every extreme that they name: Sequence b's memory holds mem_len[b] valid tokens from position 0; in every draw some sequence has all 32.
All inputs are finite; a program needn't handle non-finite values.
Results may differ from a plain program's by a relative error of at most 0.028.
The roundings to bfloat16 on the way count: a program that leaves them out, or rounds other values in their place, can miss the bound.
Values may be sent and summed in bfloat16 or wider, within the bound.
A program may use at most 64 MiB of HBM per device.

v0:
```python
import jax
import jax.numpy as jnp
from jax import lax
from jax.sharding import PartitionSpec as P

HEAD_DIM = 256


epsilon = 1e-06


def broadcast(block, axis, holder):
    block = jnp.where(lax.axis_index(axis) == holder, block, jnp.zeros_like(block))
    return lax.psum(block, axis)


def on_device(enc_state, final_gain, queries, w_key, w_value, ctx_grad, mem_len):
    sections = lax.axis_size("section")
    replicas = lax.axis_size("dp")
    section_index = lax.axis_index("section")
    last_encoder = sections // 2 - 1
    is_decoder = (section_index > last_encoder).astype(jnp.float32)
    is_last = (section_index == last_encoder).astype(jnp.float32)
    src_len = enc_state.shape[1]
    tgt_len = queries.shape[1]
    local_width = w_key.shape[2]
    heads_here = local_width // HEAD_DIM
    score_scale = HEAD_DIM ** (-0.5)
    enc_rows = enc_state[0].astype(jnp.float32)
    inverse = lax.rsqrt(jnp.mean(enc_rows * enc_rows, axis=1, keepdims=True) + epsilon)
    normed = enc_rows * inverse
    memory = (normed * final_gain).astype(jnp.bfloat16)
    sent = broadcast(memory, "section", last_encoder)
    all_memory, all_len = (
        lax.all_gather(sent, "dp", axis=0, tiled=True),
        lax.all_gather(mem_len, "dp", axis=0, tiled=True),
    )
    w_both = jnp.concatenate([w_key[0], w_value[0]], axis=1)
    projected = jnp.dot(all_memory, w_both, preferred_element_type=jnp.float32).astype(jnp.bfloat16)
    key_rows = projected[:, :local_width].reshape(replicas, src_len, heads_here, HEAD_DIM)
    value_rows = projected[:, local_width:].reshape(replicas, src_len, heads_here, HEAD_DIM)
    query_heads, grad_heads = (
        lax.all_to_all(queries[0], "dp", split_axis=1, concat_axis=0, tiled=True),
        lax.all_to_all(ctx_grad[0], "dp", split_axis=1, concat_axis=0, tiled=True),
    )
    query_rows = query_heads.reshape(replicas, tgt_len, heads_here, HEAD_DIM)
    grad_rows = grad_heads.reshape(replicas, tgt_len, heads_here, HEAD_DIM)
    key_valid = jnp.arange(src_len, dtype=jnp.int32)[None, :] < all_len[:, None]
    scores = (
        jnp.einsum("btha,buha->bhut", query_rows, key_rows, preferred_element_type=jnp.float32)
        * score_scale
    )
    scores = jnp.where(key_valid[:, None, :, None], scores, -1e30)
    row_max = jnp.max(scores, axis=2, keepdims=True)
    exponent = jnp.exp(scores - row_max)
    probs = exponent / jnp.sum(exponent, axis=2, keepdims=True)
    probs_low = probs.astype(jnp.bfloat16)
    grad_probs = jnp.einsum(
        "btha,buha->bhut", grad_rows, value_rows, preferred_element_type=jnp.float32
    )
    row_delta = jnp.sum(probs * grad_probs, axis=2, keepdims=True)
    grad_scores = (probs * (grad_probs - row_delta) * score_scale).astype(jnp.bfloat16)
    query_grad_heads = (
        jnp.einsum("bhut,buha->btha", grad_scores, key_rows, preferred_element_type=jnp.float32)
        .astype(jnp.bfloat16)
        .reshape(replicas * tgt_len, local_width)
    )
    key_grad = (
        jnp.einsum("bhut,btha->buha", grad_scores, query_rows, preferred_element_type=jnp.float32)
        .astype(jnp.bfloat16)
        .reshape(replicas * src_len, local_width)
    )
    value_grad = (
        jnp.einsum("bhut,btha->buha", probs_low, grad_rows, preferred_element_type=jnp.float32)
        .astype(jnp.bfloat16)
        .reshape(replicas * src_len, local_width)
    )
    both_grads = jnp.concatenate([key_grad, value_grad], axis=1)
    weight_grads = (
        lax.dot_general(
            all_memory, both_grads, (((0,), (0,)), ((), ())), preferred_element_type=jnp.float32
        )
        * is_decoder
    ).astype(jnp.bfloat16)
    query_back = lax.all_to_all(query_grad_heads, "dp", split_axis=0, concat_axis=1, tiled=True)
    query_grad = (query_back.astype(jnp.float32) * is_decoder).astype(jnp.bfloat16)[None]
    section_part = lax.psum_scatter(
        (
            lax.dot_general(
                both_grads, w_both, (((1,), (1,)), ((), ())), preferred_element_type=jnp.float32
            )
            * is_decoder
        ).astype(jnp.bfloat16),
        "dp",
        scatter_dimension=0,
        tiled=True,
    )
    memory_grad = lax.psum(section_part, "section").astype(jnp.float32)
    scaled_grad = memory_grad * final_gain
    last_grad = inverse * (
        scaled_grad - normed * jnp.mean(scaled_grad * normed, axis=1, keepdims=True)
    )
    state_grad = (last_grad * is_last).astype(jnp.bfloat16)[None]
    gain_grad = lax.psum(jnp.sum(memory_grad * normed, axis=0) * is_last, ("section", "dp"))
    key_weight_grad = weight_grads[:, :local_width][None]
    value_weight_grad = weight_grads[:, local_width:][None]
    return (query_grad, key_weight_grad, value_weight_grad, state_grad, gain_grad)


def solution(mesh):
    placed = (
        P("section", "dp", None),
        P(),
        P("section", "dp", None),
        P("section", None, "dp"),
        P("section", None, "dp"),
        P("section", "dp", None),
        P("dp"),
    )
    return jax.shard_map(
        on_device,
        mesh=mesh,
        in_specs=placed,
        out_specs=(
            P("section", "dp", None),
            P("section", None, "dp"),
            P("section", None, "dp"),
            P("section", "dp", None),
            P(),
        ),
        check_vma=False,
    )
```

profile of v0, /device:TPU:65, one launch (start us, length us, event | category | flops | bytes accessed | tf_op | source)
XLA Modules:
  0.0 636.4 jit_solution(12333519288310503521)
XLA Ops:
  7.2 1.2 fusion.28
  8.4 1.8 fusion.33
  10.3 146.5 %all-reduce.4.cloned.1.call-done = bf16[32,4096]{1,0:T(8,128)(2,1)} async-done(((bf16[32,4096]{1,0:T(8,128)(2,1)}), bf16[32,4096]{1,0:T(8,128)(2,1)}) %all-reduce.4.cloned.1.call-update) | async-done | bytes 262160 | tf_op jit(solution)/shard_map/psum | solution.py:14
  156.8 1.6 copy.13
  158.4 1.3 copy.14
  159.7 18.1 %all-to-all-start = ((bf16[128,16,256]{2,0,1:T(8,128)(2,1)}), bf16[128,16,256]{2,0,1:T(8,128)(2,1)S(1)}, u32[]{:S(2)}, u32[]{:S(2)}) async-start(bf16[128,16,256]{2,0,1:T(8,128)(2,1)} %copy.14), calls=%async_computation | async-start | bytes 2097152 | tf_op jit(solution)/shard_map/all_to_all | solution.py:43
  178.5 1.3 copy.16
  179.8 18.9 %all-to-all-done = bf16[128,16,256]{2,0,1:T(8,128)(2,1)S(1)} async-done(((bf16[128,16,256]{2,0,1:T(8,128)(2,1)}), bf16[128,16,256]{2,0,1:T(8,128)(2,1)S(1)}, u32[]{:S(2)}, u32[]{:S(2)}) %all-to-all-start) | async-done | bytes 1048608 | tf_op jit(solution)/shard_map/all_to_all | solution.py:43
  198.7 5.7 all-to-all-start.1
  205.6 0.8 dynamic-update-slice
  206.4 23.7 %all-reduce = s32[16]{0:T(128)S(1)} all-reduce(s32[16]{0:T(128)S(1)} %dynamic-update-slice), channel_id=1, replica_groups=mesh['section'=16,'dp'=16] {'dp'}, use_global_device_ids=true, to_apply=%add | all-reduce | flops 16 | bytes 128
  230.1 42.5 %all-gather.2.cloned.1.call-done = bf16[512,4096]{1,0:T(8,128)(2,1)} async-done(((bf16[32,4096]{1,0:T(8,128)(2,1)}), bf16[512,4096]{1,0:T(8,128)(2,1)}) %all-gather.2.cloned.1.call-update) | async-done | bytes 4194320 | tf_op jit(solution)/shard_map/all_gather | solution.py:35
  272.6 5.8 fusion.4
  280.6 6.6 %multiply_convert_fusion = bf16[512,4096]{1,0:T(8,128)(2,1)} fusion(f32[]{:T(128)S(6)} %convert_element_type.108, bf16[4096,256]{1,0:T(8,128)(2,1)} %bitcast.67, bf16[4096,256]{1,0:T(8,128)(2,1)} %bitcast.69, bf16[512,256]{1,0:T(8,128)(2,1)S(1)} %bitcast.70, bf16[512,256]{1,0:T(8,128)(2,1)S(1)} %bitcast.72), kind=kOutput, calls=%fused_computation.2 | convolution fusion | flops 2161115136 | bytes 8912900 | tf_op jit(solution)/shard_map/dot_general | solution.py:89
  287.2 1.5 fusion.3
  288.7 3.9 all-to-all-start.2
  292.7 4.6 multiply_convert_fusion.1
  297.3 2.3 slice_bitcast_fusion
  299.6 90.7 %reduce-scatter.2.cloned.1.call-done = bf16[32,4096]{1,0:T(8,128)(2,1)} async-done(((bf16[512,4096]{1,0:T(8,128)(2,1)}), bf16[32,4096]{1,0:T(8,128)(2,1)}) %reduce-scatter.2.cloned.1.call-update) | async-done | bytes 262160 | tf_op jit(solution)/shard_map/reduce_scatter | solution.py:87
  390.6 1.3 copy.17
  391.9 143.4 %all-reduce.6.cloned.1.call-done = bf16[32,4096]{1,0:T(8,128)(2,1)} async-done(((bf16[32,4096]{1,0:T(8,128)(2,1)}), bf16[32,4096]{1,0:T(8,128)(2,1)}) %all-reduce.6.cloned.1.call-update) | async-done | bytes 262160 | tf_op jit(solution)/shard_map/psum | solution.py:98
  535.3 1.3 fusion.27
  536.6 91.4 %psum.23 = f32[4096]{0:T(1024)} all-reduce(f32[4096]{0:T(1024)S(1)} %broadcast_multiply_fusion), channel_id=1, replica_groups=mesh['section'=16,'dp'=16] {'section','dp'}, use_global_device_ids=true, to_apply=%region_9.10 | all-reduce | flops 4096 | bytes 32768 | tf_op jit(solution)/shard_map/psum | solution.py:104
  628.0 1.8 fusion.34
  (32 shorter events, 4.0 us)
Async XLA Ops:
  7.2 170.6 %copy-start.1 = (bf16[1,128,4096]{2,1,0:T(8,128)(2,1)S(1)}, bf16[1,128,4096]{2,1,0:T(8,128)(2,1)}, u32[]{:S(2)}) copy-start(bf16[1,128,4096]{2,1,0:T(8,128)(2,1)} %param.12) | copy-start | bytes 3145732
  7.2 149.6 %all-reduce.4.cloned.1.call-start = ((), (), s32[]{:S(2)}) async-start(), calls=%async_computation.4 | async-start | bytes 524288 | tf_op jit(solution)/shard_map/psum | solution.py:14
  10.3 262.4 %all-gather.2.cloned.1.call-start = ((), (), s32[]{:S(2)}) async-start(), calls=%async_computation.5 | async-start | bytes 4456448 | tf_op jit(solution)/shard_map/all_gather | solution.py:35
  159.7 45.3 %copy-start.3 = (u32[256]{0:T(256)S(1)}, u32[256]{0:T(256)}, u32[]{:S(2)}) copy-start(u32[256]{0:T(256)} %constant.31) | copy-start | bytes 3076
  159.7 38.9 %all-to-all-start = ((bf16[128,16,256]{2,0,1:T(8,128)(2,1)}), bf16[128,16,256]{2,0,1:T(8,128)(2,1)S(1)}, u32[]{:S(2)}, u32[]{:S(2)}) async-start(bf16[128,16,256]{2,0,1:T(8,128)(2,1)} %copy.14), calls=%async_computation | async-start | bytes 2097152 | tf_op jit(solution)/shard_map/all_to_all | solution.py:43
  198.7 80.9 %all-to-all-start.1 = ((bf16[128,16,256]{2,0,1:T(8,128)(2,1)}), bf16[128,16,256]{2,0,1:T(8,128)(2,1)S(1)}, u32[]{:S(2)}, u32[]{:S(2)}) async-start(bf16[128,16,256]{2,0,1:T(8,128)(2,1)} %copy.16), calls=%async_computation.1 | async-start | bytes 2097152 | tf_op jit(solution)/shard_map/all_to_all | solution.py:44
  204.3 186.0 %reduce-scatter.2.cloned.1.call-start = ((), (), s32[]{:S(2)}) async-start(), calls=%async_computation.6 | async-start | bytes 4456448 | tf_op jit(solution)/shard_map/reduce_scatter | solution.py:87
  288.7 101.6 %all-to-all-start.2 = ((bf16[16,128,256]{1,2,0:T(8,128)(2,1)}), bf16[16,128,256]{1,2,0:T(8,128)(2,1)S(1)}, u32[]{:S(2)}, u32[]{:S(2)}) async-start(bf16[16,128,256]{1,2,0:T(8,128)(2,1)} %fusion.3), calls=%async_computation.2 | async-start | bytes 2097152 | tf_op jit(solution)/shard_map/all_to_all | solution.py:85
  292.6 242.7 %all-reduce.6.cloned.1.call-start = ((), (), s32[]{:S(2)}) async-start(), calls=%async_computation.7 | async-start | bytes 524288 | tf_op jit(solution)/shard_map/psum | solution.py:98
  299.6 235.7 %copy-start = (bf16[1,32,4096]{2,1,0:T(8,128)(2,1)S(1)}, bf16[1,32,4096]{2,1,0:T(8,128)(2,1)}, u32[]{:S(2)}) copy-start(bf16[1,32,4096]{2,1,0:T(8,128)(2,1)} %param.7) | copy-start | bytes 786436
  299.6 235.7 %copy-start.2 = (f32[4096]{0:T(1024)S(1)}, f32[4096]{0:T(1024)}, u32[]{:S(2)}) copy-start(f32[4096]{0:T(1024)} %param.8) | copy-start | bytes 49156
Sparse Core Ops, SparseCore 0:
  11.2 145.5 all-reduce.3
  159.5 113.0 all-gather.1
  287.4 102.8 reduce-scatter.1
  392.8 142.4 all-reduce.5
where the time goes:
time: 640 us; the launch traced here: 636 us
  waiting for transfers between devices  442 us (69%)
  blocking collectives  115 us (18%)
  starting transfers between devices  27.8 us (4%)
  matrix products  20 us (3%)
  between operations  14.6 us (2%)
  local copies, waits for them, and re-layouts  9.89 us (2%)
  other arithmetic  7.1 us (1%)
    psum x1, waiting for transfers between devices, broadcast(): return lax.psum(block, axis)  146 us
    psum x1, waiting for transfers between devices, on_device(): memory_grad = lax.psum(section_part, 'section').astype(jnp.float32)  143 us
    psum x1, blocking collectives, on_device(): lax.psum(jnp.sum(memory_grad * normed, axis=0) * is_last, ('section', 'dp'))  91.4 us
    reduce_scatter x1, waiting for transfers between devices, on_device(): lax.psum_scatter((lax.dot_general(both_grads, w_both, (((1,), (1,)), ((),...  90.7 us
    all_gather x1, waiting for transfers between devices, on_device(): lax.all_gather(sent, 'dp', axis=0, tiled=True)  42.5 us
    unnamed x1, blocking collectives  23.7 us
    all_to_all x1, waiting for transfers between devices, on_device(): lax.all_to_all(queries[0], 'dp', split_axis=1, concat_axis=0, tiled=True)  18.9 us
    all_to_all x1, starting transfers between devices, on_device(): lax.all_to_all(queries[0], 'dp', split_axis=1, concat_axis=0, tiled=True)  18.1 us
  transfers between devices with their start and end apart: 7, of which 5 were waited for; matrix products, arithmetic and copies ran while one was open for 4% of the time, Pallas kernels for 0%

commit v1 on v0

v1 whole, which is shorter than its diff:
```python
import jax
import jax.numpy as jnp
from jax import lax
from jax.experimental import pallas as pl
from jax.experimental.pallas import tpu as pltpu
from jax.sharding import PartitionSpec as P

D = 4096
HD = 256
SRC = 32
TGT = 128
SCALE = HD ** (-0.5)
EPS = 1e-06
MESH = pl.DeviceIdType.MESH
NT = (((1,), (1,)), ((), ()))
TN = (((0,), (0,)), ((), ()))
BF = jnp.bfloat16
F32 = jnp.float32


def mod(a, n):
    return lax.rem(a + n, n)


def body(
    enc, gain_in, q_in, g_in, wk_in, wv_in, mlen,
    qg_out, mem_out, kvg_out, state_out, gain_out,
    hbuf, gain, memsrc, rbuf, mem, w, qs, gs, qgs, acc, kv, kvall, kvg, kvgall,
    gacc, dsend, drecv, cs, relay, fin, rsum, peer, fchunk, zbuf, ysum, sbuf,
    g1, g1r, g2, g2r, g3r, stv, gov,
    lsem, ssem, src_s, rs, rp, kvs, kvss, gsem, gss, dss, drs, rel_s, fin_s, peer_s, z_s, y_s,
    g1s, g2s, g3s, g1ss, g2ss, g3ss,
):
    s = lax.axis_index("section")
    d = lax.axis_index("dp")
    y = lax.rem(s, 4)
    zl = s // 4
    x = d // 4
    h = lax.rem(d // 2, 2)
    c = lax.rem(d, 2)
    d_flip = d + 2 - 4 * h
    partner = d + 1 - 2 * c
    my_p = c * 8 + h * 4 + x
    is_dec = zl >= 2
    is_relay = zl == 1

    def dp_of(xx, hh):
        return xx * 4 + hh * 2 + c

    def p_of(t):
        return lax.rem(t, 2) * 8 + lax.rem(t // 2, 2) * 4 + t // 4

    def copy(src, dst, ss, rsem, dev):
        return pltpu.make_async_remote_copy(
            src_ref=src, dst_ref=dst, send_sem=ss, recv_sem=rsem, device_id=dev, device_id_type=MESH
        )

    def arrived(dst, rsem):
        copy(dst, dst, ssem.at[0], rsem, (s, partner)).wait_recv()

    bar = pltpu.get_barrier_semaphore()
    for k in range(1, 16):
        pl.semaphore_signal(bar, inc=1, device_id=(s, lax.rem(d + k, 16)), device_id_type=MESH)
    for k in range(1, 16):
        pl.semaphore_signal(bar, inc=1, device_id=(lax.rem(s + k, 16), d), device_id_type=MESH)

    @pl.when(is_relay)
    def _():
        for k in (4, 8):
            pl.semaphore_signal(bar, inc=1, device_id=(s + k, d_flip), device_id_type=MESH)

    @pl.when(is_dec)
    def _():
        pl.semaphore_signal(bar, inc=1, device_id=(4 + y, d_flip), device_id_type=MESH)

    def load(i, src, dst):
        return pltpu.make_async_copy(src, dst, lsem.at[i])

    load_gain = load(0, gain_in, gain)
    load_enc = load(1, enc, hbuf)
    load_wk = load(2, wk_in, w.at[:, pl.ds(0, HD)])
    load_wv = load(3, wv_in, w.at[:, pl.ds(HD, HD)])
    load_q = load(4, q_in, qs)
    load_g = load(5, g_in, gs)
    load_gain.start()

    def norm_parts():
        hf = hbuf[...].astype(F32)
        inv = lax.rsqrt(jnp.mean(hf * hf, axis=1, keepdims=True) + EPS)
        return inv, hf * inv

    @pl.when(s == 7)
    def _():
        load_enc.start()

    @pl.when(is_dec)
    def _():
        load_wk.start()
        load_wv.start()
        load_q.start()
        load_g.start()

    load_gain.wait()

    @pl.when(s == 7)
    def _():
        load_enc.wait()
        _, normed = norm_parts()
        memory = (normed * gain[...]).astype(BF)
        for j in range(4):
            memsrc[j] = memory[:, j * 1024 : (j + 1) * 1024]

    pl.semaphore_wait(bar, 30 + lax.rem(2 * zl, 3) + zl // 3)

    def chunk(cc, hh, xx, jj):
        return mem.at[jj, cc * 8 + hh * 4 + xx]

    def spread(src):
        sends = []
        for i, (zz, hh) in enumerate(((2, 0), (3, 0), (2, 1), (3, 1))):
            cp = copy(src, chunk(c, h, x, y), ssem.at[i], rs.at[h, x, y], (zz * 4 + y, dp_of(x, hh)))
            cp.start()
            sends.append(cp)
        return sends

    @pl.when(s == 7)
    def _():
        sends = []
        for j in (1, 0, 2):
            cp = copy(memsrc.at[j], rbuf, ssem.at[4 + j], src_s, (4 + j, d))
            cp.start()
            sends.append(cp)
        sends += spread(memsrc.at[3])
        for cp in sends:
            cp.wait_send()

    @pl.when(is_relay & (s != 7))
    def _():
        arrived(rbuf, src_s)
        for cp in spread(rbuf):
            cp.wait_send()

    @pl.when(is_dec)
    def _():
        count = [0]
        sends = []

        def send(src, dst, rsem, dev):
            cp = copy(src, dst, ssem.at[count[0]], rsem, dev)
            count[0] += 1
            cp.start()
            sends.append(cp)

        def at_y(k):
            return (zl * 4 + mod(y + k, 4), d)

        def at_x(k):
            return (s, dp_of(mod(x + k, 4), h))

        def pass_on(hh, xx, jj, devs):
            ref = chunk(c, hh, xx, jj)
            for dev in devs:
                send(ref, ref, rs.at[hh, xx, jj], dev)
            send(ref, ref, rp.at[hh, xx, jj], (s, partner))

        def got(hh, xx, jj):
            arrived(chunk(c, hh, xx, jj), rs.at[hh, xx, jj])

        got(0, x, y)
        pass_on(0, x, y, [at_x(1), at_x(-1), at_x(2), at_y(1), at_y(-1)])
        got(1, x, y)
        pass_on(1, x, y, [at_y(1), at_y(-1), at_y(2), at_x(1), at_x(-1)])
        for k in (1, -1, 2):
            got(0, mod(x + k, 4), y)
            pass_on(0, mod(x + k, 4), y, [at_y(1), at_y(-1)])
            got(1, x, mod(y + k, 4))
            pass_on(1, x, mod(y + k, 4), [at_x(1), at_x(-1)])
        for i in range(4):
            for k in (-1, 1):
                fwd = (i < 2) == (k == -1)
                got(0, i, mod(y + k, 4))
                pass_on(0, i, mod(y + k, 4), [at_y(-k)] if fwd else [])
                got(1, mod(x + k, 4), i)
                pass_on(1, mod(x + k, 4), i, [at_x(-k)] if fwd else [])
        for i in range(4):
            got(0, i, mod(y + 2, 4))
            pass_on(0, i, mod(y + 2, 4), [])
            got(1, mod(x + 2, 4), i)
            pass_on(1, mod(x + 2, 4), i, [])
        for hh in range(2):
            for i in range(4):
                for j in range(4):
                    arrived(chunk(1 - c, hh, i, j), rp.at[hh, i, j])
        save_mem = pltpu.make_async_copy(mem, mem_out, lsem.at[6])
        save_mem.start()

        load_wk.wait()
        load_wv.wait()

        acc[...] = jnp.zeros_like(acc)

        def project(j, _):
            rows = mem[j].reshape(512, 1024)
            acc[...] += jnp.dot(rows, w[pl.ds(pl.multiple_of(j * 1024, 1024), 1024), :], preferred_element_type=F32)
            return 0

        lax.fori_loop(0, 4, project, 0)
        kv[...] = acc[...].astype(BF).reshape(16, SRC, 512)

        for cp in sends:
            cp.wait_send()

        for k in range(1, 16):
            t = lax.rem(d + k, 16)
            copy(kv.at[p_of(t)], kvall.at[d], kvss.at[k], kvs.at[d], (s, t)).start()
        kvall[d] = kv[my_p]

        load_q.wait()
        load_g.wait()
        valid = lax.broadcasted_iota(jnp.int32, (SRC, TGT), 0) < mlen[0]

        def head(a):
            cols = pl.ds(pl.multiple_of(a * HD, HD), HD)
            key = kvall[a, :, 0:HD]
            value = kvall[a, :, HD : 2 * HD]
            q = qs[:, cols]
            g = gs[:, cols]
            sc = lax.dot_general(key, q, NT, preferred_element_type=F32) * SCALE
            sc = jnp.where(valid, sc, -1e30)
            e = jnp.exp(sc - jnp.max(sc, axis=0, keepdims=True))
            pr = e / jnp.sum(e, axis=0, keepdims=True)
            gp = lax.dot_general(value, g, NT, preferred_element_type=F32)
            delta = jnp.sum(pr * gp, axis=0, keepdims=True)
            gsr = (pr * (gp - delta) * SCALE).astype(BF)
            kvg[a, :, 0:HD] = jnp.dot(gsr, q, preferred_element_type=F32).astype(BF)
            kvg[a, :, HD : 2 * HD] = jnp.dot(pr.astype(BF), g, preferred_element_type=F32).astype(BF)
            qgs[:, cols] = lax.dot_general(gsr, key, TN, preferred_element_type=F32).astype(BF)

        def send_back(a):
            return copy(kvg.at[a], kvgall.at[my_p], gss.at[a], gsem.at[my_p], (s, a))

        def heads(i, _):
            for n in range(4):
                a = mod(d - (i * 4 + n), 16)

                @pl.when(a != d)
                def _():
                    arrived(kvall.at[a], kvs.at[a])

            for n in range(4):
                head(mod(d - (i * 4 + n), 16))
            for n in range(4):
                a = mod(d - (i * 4 + n), 16)

                @pl.when(a != d)
                def _():
                    send_back(a).start()

            return 0

        lax.fori_loop(0, 4, heads, 0)
        kvgall[my_p] = kvg[d]
        save_qg = pltpu.make_async_copy(qgs, qg_out, lsem.at[7])
        save_qg.start()
        for k in range(1, 16):
            t = lax.rem(d + k, 16)
            arrived(kvgall.at[p_of(t)], gsem.at[p_of(t)])
        save_kvg = pltpu.make_async_copy(kvgall, kvg_out, lsem.at[8])
        save_kvg.start()

        gacc[...] = jnp.zeros_like(gacc)
        order = [mod(y + k, 4) for k in (2, 1, -1, 0)]

        def grads(cc, j, put):
            def part(i, _):
                n0 = pl.multiple_of(i * 512, 512)
                left = kvgall[pl.ds(cc * 8, 8)].reshape(256, 512)
                wt = w[pl.ds(pl.multiple_of(j * 1024 + i * 512, 512), 512), :]
                tile = lax.dot_general(left, wt, NT, preferred_element_type=F32)
                m = mem[j, pl.ds(cc * 8, 8), :, pl.ds(n0, 512)].reshape(256, 512).astype(F32)
                gacc[j, :, pl.ds(n0, 512)] += jnp.sum((tile * m).reshape(32, 8, 512), axis=0)
                put(n0, tile.reshape(8, SRC, 512))
                return 0

            lax.fori_loop(0, 2, part, 0)

        def swap(j):
            return copy(dsend.at[j], drecv.at[j], dss.at[j], drs.at[j], (s, partner))

        for j in order:
            def put_send(n0, tile, j=j):
                dsend[j, :, :, pl.ds(n0, 512)] = tile.astype(BF)

            grads(1 - c, j, put_send)
            swap(j).start()

        count[0] = 0
        sends = []

        def cut(hh, pos, i):
            return cs.at[pos, i] if hh == 0 else cs.at[i, 4 + pos]

        def along(hh, k):
            return at_y(k) if hh == 0 else at_x(k)

        def across(hh, k):
            return at_x(k) if hh == 0 else at_y(k)

        mine = (y, x)

        def far(hh, i):
            k = 1 if i < 2 else -1
            send(cut(hh, mod(mine[hh] + 2, 4), i), relay.at[hh, i], rel_s.at[hh, i], along(hh, k))

        def near(hh, i, k):
            side = 0 if k == 1 else 1
            send(cut(hh, mod(mine[hh] + k, 4), i), fin.at[hh, side, i], fin_s.at[hh, side, i], along(hh, k))

        for j in order:
            swap(j).wait_recv()

            def put_own(n0, tile, j=j):
                cs[j, :, :, pl.ds(n0, 512)] = (tile + drecv[j, :, :, pl.ds(n0, 512)].astype(F32)).astype(BF)

            grads(c, j, put_own)
            if j is order[0]:
                for i in range(4):
                    far(0, i)
        for i in range(4):
            far(1, i)
        for hh in range(2):
            for i in range(4):
                near(hh, i, -1 if i < 2 else 1)

        for t in range(16):
            part = gacc[t // 4, :, (t % 4) * 256 : (t % 4 + 1) * 256]
            g1[t] = jnp.sum(part, axis=0, keepdims=True)
        for k in range(1, 16):
            t = lax.rem(d + k, 16)
            copy(g1.at[t], g1r.at[d], g1ss.at[k], g1s.at[d], (s, t)).start()
        g1r[d] = g1[d]

        for i in range(4):
            for hh in range(2):
                k = 1 if i < 2 else -1
                arrived(relay.at[hh, i], rel_s.at[hh, i])
                ref = cut(hh, mod(mine[hh] + k, 4), i)
                ref[...] = (ref[...].astype(F32) + relay[hh, i].astype(F32)).astype(BF)
                near(hh, i, k)

        for k in range(1, 16):
            t = lax.rem(d + k, 16)
            arrived(g1r.at[t], g1s.at[t])
        g2[...] = jnp.sum(g1r[...], axis=0)
        for k in range(1, 16):
            copy(g2, g2r.at[s - 8], g2ss.at[k], g2s.at[s - 8], (lax.rem(s + k, 16), d)).start()
        g2r[s - 8] = g2[...]

        for i in range(4):
            for hh in range(2):
                for side in range(2):
                    arrived(fin.at[hh, side, i], fin_s.at[hh, side, i])
                rsum[hh, i] = (
                    cut(hh, mine[hh], i)[...].astype(F32) + fin[hh, 0, i].astype(F32) + fin[hh, 1, i].astype(F32)
                ).astype(BF)
        other = (x, y)
        for k in (2, 1, 3):
            for hh in range(2):
                send(rsum.at[hh, mod(other[hh] + k, 4)], peer.at[hh, k - 1], peer_s.at[hh, k - 1], across(hh, k))
        for hh in range(2):
            total = rsum[hh, other[hh]].astype(F32)
            for k in range(3):
                arrived(peer.at[hh, k], peer_s.at[hh, k])
                total = total + peer[hh, k].astype(F32)
            fchunk[hh] = total.astype(BF)
            slot = (zl - 2) * 2 + h
            send(fchunk.at[hh], zbuf.at[slot], z_s.at[slot], (4 + y, dp_of(x, hh)))

        for cp in sends:
            cp.wait_send()
        for k in range(1, 16):
            t = lax.rem(d + k, 16)
            copy(kv.at[p_of(t)], kvall.at[d], kvss.at[k], kvs.at[d], (s, t)).wait_send()
            send_back(t).wait_send()
            copy(g1.at[t], g1r.at[d], g1ss.at[k], g1s.at[d], (s, t)).wait_send()
            copy(g2, g2r.at[s - 8], g2ss.at[k], g2s.at[s - 8], (lax.rem(s + k, 16), d)).wait_send()
        for j in order:
            swap(j).wait_send()
        save_mem.wait()
        save_qg.wait()
        save_kvg.wait()

    for i in range(8):
        @pl.when(s != 8 + i)
        def _(i=i):
            arrived(g2r.at[i], g2s.at[i])

    g3r[d] = jnp.sum(g2r[...], axis=0)
    for k in range(1, 16):
        copy(g3r.at[d], g3r.at[d], g3ss.at[k], g3s.at[d], (s, lax.rem(d + k, 16))).start()

    @pl.when(is_relay)
    def _():
        total = jnp.zeros((SRC, 1024), F32)
        for i in range(4):
            arrived(zbuf.at[i], z_s.at[i])
            total = total + zbuf[i].astype(F32)
        ysum[...] = total.astype(BF)

    @pl.when(is_relay & (s != 7))
    def _():
        cp = copy(ysum, sbuf.at[y], ssem.at[0], y_s.at[y], (7, d))
        cp.start()
        cp.wait_send()

    @pl.when(s == 7)
    def _():
        inv, normed = norm_parts()
        for j in range(3):
            arrived(sbuf.at[j], y_s.at[j])
        sbuf[3] = ysum[...]
        mgrad = jnp.concatenate([sbuf[j].astype(F32) for j in range(4)], axis=1)
        scaled = mgrad * gain[...]
        stv[...] = (inv * (scaled - normed * jnp.mean(scaled * normed, axis=1, keepdims=True))).astype(BF)

    @pl.when(s != 7)
    def _():
        stv[...] = jnp.zeros_like(stv)

    save_state = pltpu.make_async_copy(stv, state_out, lsem.at[6])
    save_state.start()
    for k in range(1, 16):
        t = lax.rem(d + k, 16)
        arrived(g3r.at[t], g3s.at[t])
    for t in range(16):
        gov[:, t * 256 : (t + 1) * 256] = g3r[t] / gain[:, t * 256 : (t + 1) * 256]
    save_gain = pltpu.make_async_copy(gov, gain_out, lsem.at[7])
    save_gain.start()
    for k in range(1, 16):
        copy(g3r.at[d], g3r.at[d], g3ss.at[k], g3s.at[d], (s, lax.rem(d + k, 16))).wait_send()
    save_state.wait()
    save_gain.wait()


def exchange(enc, gain, q, g, wk, wv, mlen):
    any_spec = pl.BlockSpec(memory_space=pl.ANY)
    V = pltpu.VMEM
    S = pltpu.SemaphoreType.DMA
    return pl.pallas_call(
        body,
        name="relay_attention",
        out_shape=(
            jax.ShapeDtypeStruct((TGT, D), BF),
            jax.ShapeDtypeStruct((4, 16, SRC, 1024), BF),
            jax.ShapeDtypeStruct((16, SRC, 512), BF),
            jax.ShapeDtypeStruct((SRC, D), BF),
            jax.ShapeDtypeStruct((1, D), F32),
        ),
        in_specs=[any_spec] * 6 + [pl.BlockSpec(memory_space=pltpu.SMEM)],
        out_specs=[any_spec] * 5,
        scratch_shapes=[
            V((SRC, D), BF),
            V((1, D), F32),
            V((4, SRC, 1024), BF),
            V((SRC, 1024), BF),
            V((4, 16, SRC, 1024), BF),
            V((D, 512), BF),
            V((TGT, D), BF),
            V((TGT, D), BF),
            V((TGT, D), BF),
            V((512, 512), F32),
            V((16, SRC, 512), BF),
            V((16, SRC, 512), BF),
            V((16, SRC, 512), BF),
            V((16, SRC, 512), BF),
            V((4, 8, 1024), F32),
            V((4, 8, SRC, 1024), BF),
            V((4, 8, SRC, 1024), BF),
            V((4, 8, SRC, 1024), BF),
            V((2, 4, SRC, 1024), BF),
            V((2, 2, 4, SRC, 1024), BF),
            V((2, 4, SRC, 1024), BF),
            V((2, 3, SRC, 1024), BF),
            V((2, SRC, 1024), BF),
            V((4, SRC, 1024), BF),
            V((SRC, 1024), BF),
            V((4, SRC, 1024), BF),
            V((16, 1, 256), F32),
            V((16, 1, 256), F32),
            V((1, 256), F32),
            V((8, 1, 256), F32),
            V((16, 1, 256), F32),
            V((SRC, D), BF),
            V((1, D), F32),
            S((9,)),
            S((64,)),
            S,
            S((2, 4, 4)),
            S((2, 4, 4)),
            S((16,)),
            S((16,)),
            S((16,)),
            S((16,)),
            S((4,)),
            S((4,)),
            S((2, 4)),
            S((2, 2, 4)),
            S((2, 3)),
            S((4,)),
            S((4,)),
            S((16,)),
            S((8,)),
            S((16,)),
            S((16,)),
            S((16,)),
            S((16,)),
        ],
        compiler_params=pltpu.CompilerParams(
            collective_id=0, has_side_effects=True, vmem_limit_bytes=60 * 1024 * 1024
        ),
    )(enc, gain, q, g, wk, wv, mlen)


def on_device(enc_state, final_gain, queries, w_key, w_value, ctx_grad, mem_len):
    is_dec = lax.axis_index("section") >= 8
    qg, mem, kvg, state, gain_grad = exchange(
        enc_state[0], final_gain.reshape(1, D), queries[0], ctx_grad[0], w_key[0], w_value[0], mem_len
    )
    rows = mem.reshape(4, 512, 1024)
    grads = kvg.reshape(512, 512)

    def weight_grad(cols):
        full = jnp.einsum("jrd,rn->jdn", rows, cols, preferred_element_type=F32)
        return jnp.where(is_dec, full.astype(BF), jnp.zeros((), BF)).reshape(1, D, HD)

    return (
        jnp.where(is_dec, qg, jnp.zeros((), BF))[None],
        weight_grad(grads[:, :HD]),
        weight_grad(grads[:, HD:]),
        state[None],
        gain_grad.reshape(D),
    )


def solution(mesh):
    placed = (
        P("section", "dp", None),
        P(),
        P("section", "dp", None),
        P("section", None, "dp"),
        P("section", None, "dp"),
        P("section", "dp", None),
        P("dp"),
    )
    return jax.shard_map(
        on_device,
        mesh=mesh,
        in_specs=placed,
        out_specs=(
            P("section", "dp", None),
            P("section", None, "dp"),
            P("section", None, "dp"),
            P("section", "dp", None),
            P(),
        ),
        check_vma=False,
    )
```

time: 640 us -> 104 us (0.16)
  waiting for transfers between devices: 442 us -> 0 us
  blocking collectives: 115 us -> 0 us
  Pallas kernels: 0 us -> 91.1 us
  starting transfers between devices: 27.8 us -> 0 us
  between operations: 14.6 us -> 1.31 us
  matrix products: 20 us -> 7.66 us
  local copies, waits for them, and re-layouts: 9.89 us -> 1.32 us
    psum x2 -> x0, waiting for transfers between devices: 290 us -> none  [the longest x1 146 us: broadcast(): return lax.psum(block, axis)]
    psum x1 -> x0, blocking collectives: 91.4 us -> none  [on_device(): lax.psum(jnp.sum(memory_grad * normed, axis=0) * is_last, ('section', 'dp'))]
    pallas_call x0 -> x1, Pallas kernels: none -> 91.1 us  [exchange(): pl.pallas_call(body, name='relay_attention', out_shape=(jax.ShapeDtypeStr...]
    reduce_scatter x1 -> x0, waiting for transfers between devices: 90.7 us -> none  [on_device(): lax.psum_scatter((lax.dot_general(both_grads, w_both, (((1,), (1,)), ((),...]
    all_gather x1 -> x0, waiting for transfers between devices: 42.5 us -> none  [on_device(): lax.all_gather(sent, 'dp', axis=0, tiled=True)]
    all_to_all x3 -> x0, starting transfers between devices: 27.7 us -> none  [the longest x1 18.1 us: on_device(): lax.all_to_all(queries[0], 'dp', split_axis=1, concat_axis=0, tiled=True)]
    unnamed x1 -> x0, blocking collectives: 23.7 us -> none
    all_to_all x3 -> x0, waiting for transfers between devices: 18.9 us -> none  [the longest x1 18.9 us: on_device(): lax.all_to_all(queries[0], 'dp', split_axis=1, concat_axis=0, tiled=True)]
  transfers between devices with their start and end apart: 7 -> 0, of which waited for: 5 -> 0; matrix products, arithmetic and copies ran while one was open for 4% -> 0% of each run, Pallas kernels for 0% -> 0%
where the time goes in v1:
time: 104 us
  Pallas kernels  91.1 us (88%)
  matrix products  7.66 us (7%)
  other arithmetic  2.33 us (2%)
  local copies, waits for them, and re-layouts  1.32 us (1%)
  between operations  1.31 us (1%)
    pallas_call x1, Pallas kernels, exchange(): pl.pallas_call(body, name='relay_attention', out_shape=(jax.ShapeDtypeStr...  91.1 us
    dot_general x2, matrix products, weight_grad(): full = jnp.einsum('jrd,rn->jdn', rows, cols, preferred_element_type=F32)  7.66 us
    broadcast_in_dim x1, other arithmetic, on_device(): jnp.where(is_dec, qg, jnp.zeros((), BF))[None]  2.33 us

profile of v1, /device:TPU:65, one launch (start us, length us, event | category | flops | bytes accessed | tf_op | source)
XLA Modules:
  0.0 103.7 jit_solution(7673552184343505111)
XLA Ops:
  1.3 91.1 %relay_attention.1 = (bf16[128,4096]{1,0:T(8,128)(2,1)}, bf16[4,16,32,1024]{3,2,1,0:T(8,128)(2,1)}, bf16[16,32,512]{2,1,0:T(8,128)(2,1)}, bf16[32,4096]{1,0:T(8,128)(2,1)}, f32[1,4096]{1,0:T(1,128)}) custom-call(bf16[32,4096]{1,0:T(8,128)(2,1)} %bitcast.27, f32[1,4096]{1,0:T(1,128)} %bitcast.28, bf16[128,4096]{1,0:T(8,128)(2,1)} %bitcast.24, ...), custom_call_target="tpu_custom_call" | custom-call | tf_op jit(solution)/shard_map/relay_attention/pallas_call | solution.py:449
  92.4 0.0 copy-start.3
  92.4 2.3 %select_bitcast_fusion = bf16[1,128,4096]{2,1,0:T(8,128)(2,1)} fusion(bf16[128,4096]{1,0:T(8,128)(2,1)} %get-tuple-element.10, pred[]{:T(512)S(6)} %ge.3), kind=kLoop, calls=%fused_computation.2 | loop fusion | flops 524288 | bytes 2097153 | tf_op jit(solution)/shard_map/broadcast_in_dim | solution.py:537
  94.7 0.0 copy-done.3
  94.7 0.0 copy-start.2
  94.7 5.0 %convert_select_fusion = bf16[4,1024,256]{2,1,0:T(8,128)(2,1)} fusion(pred[]{:T(512)S(6)} %ge.3, bf16[4,512,1024]{2,1,0:T(8,128)(2,1)} %bitcast.30, bf16[512,512]{1,0:T(8,128)(2,1)S(1)} %bitcast.32), kind=kOutput, calls=%fused_computation | convolution fusion | flops 1075838976 | bytes 6553601 | tf_op jit(solution)/shard_map/jrd,rn->jdn/dot_general | solution.py:533
  99.7 0.0 copy-done.2
  99.7 0.0 copy-start
  99.7 0.0 copy-start.1
  99.7 2.7 %convert_select_fusion.1 = bf16[4,1024,256]{2,1,0:T(8,128)(2,1)} fusion(pred[]{:T(512)S(6)} %ge.3, bf16[4,512,1024]{2,1,0:T(8,128)(2,1)S(1)} %bitcast.31, bf16[512,512]{1,0:T(8,128)(2,1)S(1)} %bitcast.33), kind=kOutput, calls=%fused_computation.1 | convolution fusion | flops 1075838976 | bytes 6553601 | tf_op jit(solution)/shard_map/jrd,rn->jdn/dot_general | solution.py:533
  102.4 0.0 copy-done
  102.4 0.7 copy.19
  103.1 0.0 copy-done.1
  103.1 0.6 copy.20
Async XLA Ops:
  92.4 2.3 %copy-start.3 = (bf16[16,32,512]{2,1,0:T(8,128)(2,1)S(1)}, bf16[16,32,512]{2,1,0:T(8,128)(2,1)}, u32[]{:S(2)}) copy-start(bf16[16,32,512]{2,1,0:T(8,128)(2,1)} %get-tuple-element.12) | copy-start | bytes 1572868
  94.7 5.0 %copy-start.2 = (bf16[4,16,32,1024]{3,2,1,0:T(8,128)(2,1)S(1)}, bf16[4,16,32,1024]{3,2,1,0:T(8,128)(2,1)}, u32[]{:S(2)}) copy-start(bf16[4,16,32,1024]{3,2,1,0:T(8,128)(2,1)} %get-tuple-element.11) | copy-start | bytes 12582916
  99.7 2.7 %copy-start = (bf16[32,4096]{1,0:T(8,128)(2,1)S(1)}, bf16[32,4096]{1,0:T(8,128)(2,1)}, u32[]{:S(2)}) copy-start(bf16[32,4096]{1,0:T(8,128)(2,1)} %get-tuple-element.13) | copy-start | bytes 786436
  99.7 3.4 %copy-start.1 = (f32[1,4096]{1,0:T(1,128)S(1)}, f32[1,4096]{1,0:T(1,128)}, u32[]{:S(2)}) copy-start(f32[1,4096]{1,0:T(1,128)} %get-tuple-element.14) | copy-start | bytes 49156

commit v2 on v1

--- a/solution.py
+++ b/solution.py
@@ -11,6 +11,8 @@
 TGT = 128
 SCALE = HD ** (-0.5)
 EPS = 1e-06
+PARTS = 2
+ROWS = SRC // PARTS
 MESH = pl.DeviceIdType.MESH
 NT = (((1,), (1,)), ((), ()))
 TN = (((0,), (0,)), ((), ()))
@@ -115,10 +117,15 @@
     def chunk(cc, hh, xx, jj):
         return mem.at[jj, cc * 8 + hh * 4 + xx]
 
-    def spread(src):
+    def piece(ref, f):
+        return ref.at[pl.ds(f * ROWS, ROWS)]
+
+    def spread(src, f):
         sends = []
         for i, (zz, hh) in enumerate(((2, 0), (3, 0), (2, 1), (3, 1))):
-            cp = copy(src, chunk(c, h, x, y), ssem.at[i], rs.at[h, x, y], (zz * 4 + y, dp_of(x, hh)))
+            cp = copy(
+                piece(src, f), piece(chunk(c, h, x, y), f), ssem.at[4 * f + i], rs.at[h, x, y, f], (zz * 4 + y, dp_of(x, hh))
+            )
             cp.start()
             sends.append(cp)
         return sends
@@ -126,18 +133,23 @@
     @pl.when(s == 7)
     def _():
         sends = []
-        for j in (1, 0, 2):
-            cp = copy(memsrc.at[j], rbuf, ssem.at[4 + j], src_s, (4 + j, d))
-            cp.start()
-            sends.append(cp)
-        sends += spread(memsrc.at[3])
+        for f in range(PARTS):
+            for j in (1, 0, 2):
+                cp = copy(piece(memsrc.at[j], f), piece(rbuf, f), ssem.at[16 + 4 * f + j], src_s.at[f], (4 + j, d))
+                cp.start()
+                sends.append(cp)
+        for f in range(PARTS):
+            sends += spread(memsrc.at[3], f)
         for cp in sends:
             cp.wait_send()
 
     @pl.when(is_relay & (s != 7))
     def _():
-        arrived(rbuf, src_s)
-        for cp in spread(rbuf):
+        sends = []
+        for f in range(PARTS):
+            arrived(piece(rbuf, f), src_s.at[f])
+            sends += spread(rbuf, f)
+        for cp in sends:
             cp.wait_send()
 
     @pl.when(is_dec)
@@ -157,63 +169,78 @@
         def at_x(k):
             return (s, dp_of(mod(x + k, 4), h))
 
-        def pass_on(hh, xx, jj, devs):
-            ref = chunk(c, hh, xx, jj)
+        def pass_on(hh, xx, jj, f, devs):
+            ref = piece(chunk(c, hh, xx, jj), f)
             for dev in devs:
-                send(ref, ref, rs.at[hh, xx, jj], dev)
-            send(ref, ref, rp.at[hh, xx, jj], (s, partner))
-
-        def got(hh, xx, jj):
-            arrived(chunk(c, hh, xx, jj), rs.at[hh, xx, jj])
-
-        got(0, x, y)
-        pass_on(0, x, y, [at_x(1), at_x(-1), at_x(2), at_y(1), at_y(-1)])
-        got(1, x, y)
-        pass_on(1, x, y, [at_y(1), at_y(-1), at_y(2), at_x(1), at_x(-1)])
-        for k in (1, -1, 2):
-            got(0, mod(x + k, 4), y)
-            pass_on(0, mod(x + k, 4), y, [at_y(1), at_y(-1)])
-            got(1, x, mod(y + k, 4))
-            pass_on(1, x, mod(y + k, 4), [at_x(1), at_x(-1)])
-        for i in range(4):
-            for k in (-1, 1):
-                fwd = (i < 2) == (k == -1)
-                got(0, i, mod(y + k, 4))
-                pass_on(0, i, mod(y + k, 4), [at_y(-k)] if fwd else [])
-                got(1, mod(x + k, 4), i)
-                pass_on(1, mod(x + k, 4), i, [at_x(-k)] if fwd else [])
-        for i in range(4):
-            got(0, i, mod(y + 2, 4))
-            pass_on(0, i, mod(y + 2, 4), [])
-            got(1, mod(x + 2, 4), i)
-            pass_on(1, mod(x + 2, 4), i, [])
-        for hh in range(2):
-            for i in range(4):
-                for j in range(4):
-                    arrived(chunk(1 - c, hh, i, j), rp.at[hh, i, j])
+                send(ref, ref, rs.at[hh, xx, jj, f], dev)
+            send(ref, ref, rp.at[hh, xx, jj, f], (s, partner))
+
+        def got(hh, xx, jj, f):
+            arrived(piece(chunk(c, hh, xx, jj), f), rs.at[hh, xx, jj, f])
+
+        for f in range(PARTS):
+            got(0, x, y, f)
+            pass_on(0, x, y, f, [at_x(1), at_x(-1), at_x(2), at_y(1), at_y(-1)])
+            got(1, x, y, f)
+            pass_on(1, x, y, f, [at_y(1), at_y(-1), at_y(2), at_x(1), at_x(-1)])
+        for f in range(PARTS):
+            for k in (1, -1, 2):
+                got(0, mod(x + k, 4), y, f)
+                pass_on(0, mod(x + k, 4), y, f, [at_y(1), at_y(-1)])
+                got(1, x, mod(y + k, 4), f)
+                pass_on(1, x, mod(y + k, 4), f, [at_x(1), at_x(-1)])
+        for f in range(PARTS):
+            for k0 in (0, 1, -1, 2):
+                for k in (-1, 1):
+                    fwd = (k0 in (0, -1)) == (k == -1)
+                    got(0, mod(x + k0, 4), mod(y + k, 4), f)
+                    pass_on(0, mod(x + k0, 4), mod(y + k, 4), f, [at_y(-k)] if fwd else [])
+                    got(1, mod(x + k, 4), mod(y + k0, 4), f)
+                    pass_on(1, mod(x + k, 4), mod(y + k0, 4), f, [at_x(-k)] if fwd else [])
+        for f in range(PARTS):
+            for k0 in (0, 1, -1, 2):
+                got(0, mod(x + k0, 4), mod(y + 2, 4), f)
+                pass_on(0, mod(x + k0, 4), mod(y + 2, 4), f, [])
+                got(1, mod(x + 2, 4), mod(y + k0, 4), f)
+                pass_on(1, mod(x + 2, 4), mod(y + k0, 4), f, [])
+
+        load_wk.wait()
+        load_wv.wait()
+
+        def project(cc):
+            acc[...] = jnp.zeros_like(acc)
+
+            def step(j, _):
+                rows = mem[j, pl.ds(cc * 8, 8)].reshape(256, 1024)
+                wj = w[pl.ds(pl.multiple_of(j * 1024, 1024), 1024), :]
+                acc[...] += jnp.dot(rows, wj, preferred_element_type=F32)
+                return 0
+
+            lax.fori_loop(0, 4, step, 0)
+            kv[pl.ds(cc * 8, 8)] = acc[...].astype(BF).reshape(8, SRC, 512)
+
+        def send_kv(t):
+            return copy(kv.at[p_of(t)], kvall.at[d], kvss.at[t], kvs.at[d], (s, t))
+
+        def other(k, cc):
+            return 2 * lax.rem(d // 2 + k, 8) + cc
+
+        project(c)
+        for k in range(1, 8):
+            send_kv(other(k, c)).start()
+        kvall[d] = kv[my_p]
+        for f in range(PARTS):
+            for hh in range(2):
+                for i in range(4):
+                    for j in range(4):
+                        arrived(piece(chunk(1 - c, hh, i, j), f), rp.at[hh, i, j, f])
         save_mem = pltpu.make_async_copy(mem, mem_out, lsem.at[6])
         save_mem.start()
-
-        load_wk.wait()
-        load_wv.wait()
-
-        acc[...] = jnp.zeros_like(acc)
-
-        def project(j, _):
-            rows = mem[j].reshape(512, 1024)
-            acc[...] += jnp.dot(rows, w[pl.ds(pl.multiple_of(j * 1024, 1024), 1024), :], preferred_element_type=F32)
-            return 0
-
-        lax.fori_loop(0, 4, project, 0)
-        kv[...] = acc[...].astype(BF).reshape(16, SRC, 512)
-
+        project(1 - c)
+        for k in range(8):
+            send_kv(other(k, 1 - c)).start()
         for cp in sends:
             cp.wait_send()
-
-        for k in range(1, 16):
-            t = lax.rem(d + k, 16)
-            copy(kv.at[p_of(t)], kvall.at[d], kvss.at[k], kvs.at[d], (s, t)).start()
-        kvall[d] = kv[my_p]
 
         load_q.wait()
         load_g.wait()
@@ -240,20 +267,18 @@
             return copy(kvg.at[a], kvgall.at[my_p], gss.at[a], gsem.at[my_p], (s, a))
 
         def heads(i, _):
-            for n in range(4):
-                a = mod(d - (i * 4 + n), 16)
-
+            cc = c + i // 2 - 2 * c * (i // 2)
+            ids = [2 * mod(d // 2 - lax.rem(i * 4 + n, 8), 8) + cc for n in range(4)]
+            for a in ids:
                 @pl.when(a != d)
-                def _():
+                def _(a=a):
                     arrived(kvall.at[a], kvs.at[a])
 
-            for n in range(4):
-                head(mod(d - (i * 4 + n), 16))
-            for n in range(4):
-                a = mod(d - (i * 4 + n), 16)
-
+            for a in ids:
+                head(a)
+            for a in ids:
                 @pl.when(a != d)
-                def _():
+                def _(a=a):
                     send_back(a).start()
 
             return 0
@@ -287,12 +312,20 @@
         def swap(j):
             return copy(dsend.at[j], drecv.at[j], dss.at[j], drs.at[j], (s, partner))
 
-        for j in order:
-            def put_send(n0, tile, j=j):
+        def partner_rows(j):
+            def put(n0, tile):
                 dsend[j, :, :, pl.ds(n0, 512)] = tile.astype(BF)
 
-            grads(1 - c, j, put_send)
+            grads(1 - c, j, put)
             swap(j).start()
+
+        def own_rows(j):
+            swap(j).wait_recv()
+
+            def put(n0, tile):
+                cs[j, :, :, pl.ds(n0, 512)] = (tile + drecv[j, :, :, pl.ds(n0, 512)].astype(F32)).astype(BF)
+
+            grads(c, j, put)
 
         count[0] = 0
         sends = []
@@ -309,28 +342,31 @@
         mine = (y, x)
 
         def far(hh, i):
-            k = 1 if i < 2 else -1
+            k = 1 - 2 * (i // 2)
             send(cut(hh, mod(mine[hh] + 2, 4), i), relay.at[hh, i], rel_s.at[hh, i], along(hh, k))
 
         def near(hh, i, k):
-            side = 0 if k == 1 else 1
+            side = (1 - k) // 2
             send(cut(hh, mod(mine[hh] + k, 4), i), fin.at[hh, side, i], fin_s.at[hh, side, i], along(hh, k))
 
-        for j in order:
-            swap(j).wait_recv()
-
-            def put_own(n0, tile, j=j):
-                cs[j, :, :, pl.ds(n0, 512)] = (tile + drecv[j, :, :, pl.ds(n0, 512)].astype(F32)).astype(BF)
-
-            grads(c, j, put_own)
-            if j is order[0]:
+        partner_rows(order[0])
+        for n in range(4):
+            j = order[n]
+            if n < 3:
+                partner_rows(order[n + 1])
+            own_rows(j)
+            if n == 0:
                 for i in range(4):
                     far(0, i)
+            if n == 1:
+                near(0, 2, 1)
+                near(0, 3, 1)
+            if n == 2:
+                near(0, 0, -1)
+                near(0, 1, -1)
+            far(1, j)
         for i in range(4):
-            far(1, i)
-        for hh in range(2):
-            for i in range(4):
-                near(hh, i, -1 if i < 2 else 1)
+            near(1, i, -1 if i < 2 else 1)
 
         for t in range(16):
             part = gacc[t // 4, :, (t % 4) * 256 : (t % 4 + 1) * 256]
@@ -348,6 +384,17 @@
                 ref[...] = (ref[...].astype(F32) + relay[hh, i].astype(F32)).astype(BF)
                 near(hh, i, k)
 
+        for i in range(4):
+            for hh in range(2):
+                for side in range(2):
+                    arrived(fin.at[hh, side, i], fin_s.at[hh, side, i])
+                rsum[hh, i] = (
+                    cut(hh, mine[hh], i)[...].astype(F32) + fin[hh, 0, i].astype(F32) + fin[hh, 1, i].astype(F32)
+                ).astype(BF)
+        cross = (x, y)
+        for k in (2, 1, 3):
+            for hh in range(2):
+                send(rsum.at[hh, mod(cross[hh] + k, 4)], peer.at[hh, k - 1], peer_s.at[hh, k - 1], across(hh, k))
         for k in range(1, 16):
             t = lax.rem(d + k, 16)
             arrived(g1r.at[t], g1s.at[t])
@@ -356,19 +403,8 @@
             copy(g2, g2r.at[s - 8], g2ss.at[k], g2s.at[s - 8], (lax.rem(s + k, 16), d)).start()
         g2r[s - 8] = g2[...]
 
-        for i in range(4):
-            for hh in range(2):
-                for side in range(2):
-                    arrived(fin.at[hh, side, i], fin_s.at[hh, side, i])
-                rsum[hh, i] = (
-                    cut(hh, mine[hh], i)[...].astype(F32) + fin[hh, 0, i].astype(F32) + fin[hh, 1, i].astype(F32)
-                ).astype(BF)
-        other = (x, y)
-        for k in (2, 1, 3):
-            for hh in range(2):
-                send(rsum.at[hh, mod(other[hh] + k, 4)], peer.at[hh, k - 1], peer_s.at[hh, k - 1], across(hh, k))
         for hh in range(2):
-            total = rsum[hh, other[hh]].astype(F32)
+            total = rsum[hh, cross[hh]].astype(F32)
             for k in range(3):
                 arrived(peer.at[hh, k], peer_s.at[hh, k])
                 total = total + peer[hh, k].astype(F32)
@@ -380,7 +416,7 @@
             cp.wait_send()
         for k in range(1, 16):
             t = lax.rem(d + k, 16)
-            copy(kv.at[p_of(t)], kvall.at[d], kvss.at[k], kvs.at[d], (s, t)).wait_send()
+            send_kv(t).wait_send()
             send_back(t).wait_send()
             copy(g1.at[t], g1r.at[d], g1ss.at[k], g1s.at[d], (s, t)).wait_send()
             copy(g2, g2r.at[s - 8], g2ss.at[k], g2s.at[s - 8], (lax.rem(s + k, 16), d)).wait_send()
@@ -468,7 +504,7 @@
             V((TGT, D), BF),
             V((TGT, D), BF),
             V((TGT, D), BF),
-            V((512, 512), F32),
+            V((256, 512), F32),
             V((16, SRC, 512), BF),
             V((16, SRC, 512), BF),
             V((16, SRC, 512), BF),
@@ -493,10 +529,10 @@
             V((SRC, D), BF),
             V((1, D), F32),
             S((9,)),
-            S((64,)),
-            S,
-            S((2, 4, 4)),
-            S((2, 4, 4)),
+            S((62 * PARTS,)),
+            S((PARTS,)),
+            S((2, 4, 4, PARTS)),
+            S((2, 4, 4, PARTS)),
             S((16,)),
             S((16,)),
             S((16,)),
@@ -521,25 +557,110 @@
     )(enc, gain, q, g, wk, wv, mlen)
 
 
+def finish(
+    qg_in, mem_in, kvg_in, state_in, gain_in,
+    qg_out, kw_out, vw_out, state_out, gain_out,
+    qg, mem, kvg, state, gain, kw, vw, ins, outs,
+):
+    is_dec = lax.axis_index("section") >= 8
+
+    def into(i, src, dst):
+        return pltpu.make_async_copy(src, dst, ins.at[i])
+
+    def out(i, src, dst):
+        return pltpu.make_async_copy(src, dst, outs.at[i])
+
+    in_state, in_gain = into(0, state_in, state), into(1, gain_in, gain)
+    out_state, out_gain = out(0, state, state_out), out(1, gain, gain_out)
+
+    def store(j):
+        rows = pl.ds(j * 1024, 1024)
+        return out(2 + j, kw.at[rows], kw_out.at[rows]), out(6 + j, vw.at[rows], vw_out.at[rows])
+
+    out_qg = out(10, qg, qg_out)
+
+    @pl.when(is_dec)
+    def _():
+        in_kvg, in_qg = into(2, kvg_in, kvg), into(3, qg_in, qg)
+        in_mem = [into(4 + j, mem_in.at[j], mem.at[j]) for j in range(4)]
+        in_kvg.start()
+        for cp in in_mem:
+            cp.start()
+        in_qg.start()
+        in_state.start()
+        in_gain.start()
+        in_kvg.wait()
+        for j in range(4):
+            in_mem[j].wait()
+            rows = mem[j].reshape(512, 1024)
+            both = lax.dot_general(rows, kvg[...].reshape(512, 512), TN, preferred_element_type=F32).astype(BF)
+            kw[j * 1024 : (j + 1) * 1024] = both[:, :HD]
+            vw[j * 1024 : (j + 1) * 1024] = both[:, HD:]
+            for cp in store(j):
+                cp.start()
+        in_qg.wait()
+        out_qg.start()
+
+    @pl.when(jnp.logical_not(is_dec))
+    def _():
+        in_state.start()
+        in_gain.start()
+        qg[...] = jnp.zeros_like(qg)
+        out_qg.start()
+        kw[...] = jnp.zeros_like(kw)
+        vw[...] = jnp.zeros_like(vw)
+        for j in range(4):
+            for cp in store(j):
+                cp.start()
+
+    in_state.wait()
+    out_state.start()
+    in_gain.wait()
+    out_gain.start()
+    for j in range(4):
+        for cp in store(j):
+            cp.wait()
+    for cp in (out_qg, out_state, out_gain):
+        cp.wait()
+
+
+def weight_grads(qg, mem, kvg, state, gain_grad):
+    any_spec = pl.BlockSpec(memory_space=pl.ANY)
+    V = pltpu.VMEM
+    S = pltpu.SemaphoreType.DMA
+    return pl.pallas_call(
+        finish,
+        name="weight_grads",
+        out_shape=(
+            jax.ShapeDtypeStruct((TGT, D), BF),
+            jax.ShapeDtypeStruct((D, HD), BF),
+            jax.ShapeDtypeStruct((D, HD), BF),
+            jax.ShapeDtypeStruct((SRC, D), BF),
+            jax.ShapeDtypeStruct((1, D), F32),
+        ),
+        in_specs=[any_spec] * 5,
+        out_specs=[any_spec] * 5,
+        scratch_shapes=[
+            V((TGT, D), BF),
+            V((4, 16, SRC, 1024), BF),
+            V((16, SRC, 512), BF),
+            V((SRC, D), BF),
+            V((1, D), F32),
+            V((D, HD), BF),
+            V((D, HD), BF),
+            S((8,)),
+            S((11,)),
+        ],
+        compiler_params=pltpu.CompilerParams(vmem_limit_bytes=60 * 1024 * 1024),
+    )(qg, mem, kvg, state, gain_grad)
+
+
 def on_device(enc_state, final_gain, queries, w_key, w_value, ctx_grad, mem_len):
-    is_dec = lax.axis_index("section") >= 8
-    qg, mem, kvg, state, gain_grad = exchange(
+    parts = exchange(
         enc_state[0], final_gain.reshape(1, D), queries[0], ctx_grad[0], w_key[0], w_value[0], mem_len
     )
-    rows = mem.reshape(4, 512, 1024)
-    grads = kvg.reshape(512, 512)
-
-    def weight_grad(cols):
-        full = jnp.einsum("jrd,rn->jdn", rows, cols, preferred_element_type=F32)
-        return jnp.where(is_dec, full.astype(BF), jnp.zeros((), BF)).reshape(1, D, HD)
-
-    return (
-        jnp.where(is_dec, qg, jnp.zeros((), BF))[None],
-        weight_grad(grads[:, :HD]),
-        weight_grad(grads[:, HD:]),
-        state[None],
-        gain_grad.reshape(D),
-    )
+    qg, kw, vw, state, gain_grad = weight_grads(*parts)
+    return qg[None], kw[None], vw[None], state[None], gain_grad.reshape(D)
 
 
 def solution(mesh):

time: 104 us -> 94.8 us (0.912)
  matrix products: 7.66 us -> 0 us
  other arithmetic: 2.33 us -> 0 us
  Pallas kernels: 91.1 us -> 93.4 us
  local copies, waits for them, and re-layouts: 1.32 us -> 0 us
    dot_general x2 -> x0, matrix products: 7.66 us -> none  [weight_grad(): full = jnp.einsum('jrd,rn->jdn', rows, cols, preferred_element_type=F32)]
    pallas_call x0 -> x1, Pallas kernels: none -> 5.94 us  [weight_grads(): pl.pallas_call(finish, name='weight_grads', out_shape=(jax.ShapeDtypeStru...]
    pallas_call x1, Pallas kernels: 91.1 us -> 87.5 us  [exchange(): pl.pallas_call(body, name='relay_attention', out_shape=(jax.ShapeDtypeStr...]
    broadcast_in_dim x1 -> x0, other arithmetic: 2.33 us -> none  [on_device(): jnp.where(is_dec, qg, jnp.zeros((), BF))[None]]
    unnamed x10 -> x0, local copies, waits for them, and re-layouts: 1.32 us -> none
where the time goes in v2:
time: 94.8 us; the launch traced here: 94.7 us
  Pallas kernels  93.4 us (99%)
  between operations  1.29 us (1%)
    pallas_call x1, Pallas kernels, exchange(): pl.pallas_call(body, name='relay_attention', out_shape=(jax.ShapeDtypeStr...  87.5 us
    pallas_call x1, Pallas kernels, weight_grads(): pl.pallas_call(finish, name='weight_grads', out_shape=(jax.ShapeDtypeStru...  5.94 us

profile of v2, /device:TPU:65, one launch (start us, length us, event | category | flops | bytes accessed | tf_op | source)
XLA Modules:
  0.0 94.7 jit_solution(5993738296416331465)
XLA Ops:
  1.3 87.5 %relay_attention.1 = (bf16[128,4096]{1,0:T(8,128)(2,1)}, bf16[4,16,32,1024]{3,2,1,0:T(8,128)(2,1)}, bf16[16,32,512]{2,1,0:T(8,128)(2,1)}, bf16[32,4096]{1,0:T(8,128)(2,1)}, f32[1,4096]{1,0:T(1,128)}) custom-call(bf16[32,4096]{1,0:T(8,128)(2,1)} %bitcast.15, f32[1,4096]{1,0:T(1,128)} %bitcast.16, bf16[128,4096]{1,0:T(8,128)(2,1)} %bitcast.13, ...), custom_call_target="tpu_custom_call" | custom-call | tf_op jit(solution)/shard_map/relay_attention/pallas_call | solution.py:485
  88.7 5.9 %weight_grads.1 = (bf16[128,4096]{1,0:T(8,128)(2,1)}, bf16[4096,256]{1,0:T(8,128)(2,1)}, bf16[4096,256]{1,0:T(8,128)(2,1)}, bf16[32,4096]{1,0:T(8,128)(2,1)}, f32[1,4096]{1,0:T(1,128)}) custom-call(bf16[128,4096]{1,0:T(8,128)(2,1)} %get-tuple-element.15.qg_in, bf16[4,16,32,1024]{3,2,1,0:T(8,128)(2,1)} %get-tuple-element.16.mem_in, ...), custom_call_target="tpu_custom_call" | custom-call | tf_op jit(solution)/shard_map/weight_grads/pallas_call | solution.py:631

commit v3 on v2

v3 whole, which is shorter than its diff:
```python
import jax
import jax.numpy as jnp
from jax import lax
from jax.experimental import pallas as pl
from jax.experimental.pallas import tpu as pltpu
from jax.sharding import PartitionSpec as P

D = 4096
HD = 256
SRC = 32
TGT = 128
SCALE = HD ** (-0.5)
EPS = 1e-06
PARTS = 2
ROWS = SRC // PARTS
MESH = pl.DeviceIdType.MESH
NT = (((1,), (1,)), ((), ()))
TN = (((0,), (0,)), ((), ()))
BF = jnp.bfloat16
F32 = jnp.float32


def mod(a, n):
    return lax.rem(a + n, n)


def body(
    enc, gain_in, q_in, g_in, wk_in, wv_in, mlen,
    qg_out, mem_out, kvg_out, state_out, gain_out,
    hbuf, gain, memsrc, rbuf, mem, w, qs, gs, qgs, acc, kv, kvall, kvg, kvgall,
    gacc, dsend, drecv, cs, relay, fin, rsum, peer, fchunk, zbuf, ysum, sbuf,
    g1, g1r, g2, g2r, g3r, stv,
    lsem, ssem, src_s, rs, far_s, rp, kvs, kvss, gsem, gss, dss, drs, rel_s, fin_s, peer_s, z_s, y_s,
    g1s, g2s, g3s, g1ss, g2ss, g3ss,
):
    s = lax.axis_index("section")
    d = lax.axis_index("dp")
    y = lax.rem(s, 4)
    zl = s // 4
    x = d // 4
    h = lax.rem(d // 2, 2)
    c = lax.rem(d, 2)
    d_flip = d + 2 - 4 * h
    partner = d + 1 - 2 * c
    my_p = c * 8 + h * 4 + x
    is_dec = zl >= 2
    is_relay = zl == 1

    def dp_of(xx, hh):
        return xx * 4 + hh * 2 + c

    def p_of(t):
        return lax.rem(t, 2) * 8 + lax.rem(t // 2, 2) * 4 + t // 4

    def copy(src, dst, ss, rsem, dev):
        return pltpu.make_async_remote_copy(
            src_ref=src, dst_ref=dst, send_sem=ss, recv_sem=rsem, device_id=dev, device_id_type=MESH
        )

    def sent(ref, sem):
        copy(ref, ref, sem, sem, (s, partner)).wait_send()

    def arrived(dst, rsem):
        copy(dst, dst, ssem.at[0], rsem, (s, partner)).wait_recv()

    bar = pltpu.get_barrier_semaphore()
    for k in range(1, 16):
        pl.semaphore_signal(bar, inc=1, device_id=(s, lax.rem(d + k, 16)), device_id_type=MESH)
    for k in range(1, 16):
        pl.semaphore_signal(bar, inc=1, device_id=(lax.rem(s + k, 16), d), device_id_type=MESH)

    @pl.when(is_relay)
    def _():
        for k in (4, 8):
            pl.semaphore_signal(bar, inc=1, device_id=(s + k, d_flip), device_id_type=MESH)

    @pl.when(is_dec)
    def _():
        pl.semaphore_signal(bar, inc=1, device_id=(4 + y, d_flip), device_id_type=MESH)

    def load(i, src, dst):
        return pltpu.make_async_copy(src, dst, lsem.at[i])

    load_gain = load(0, gain_in, gain)
    load_enc = load(1, enc, hbuf)
    load_wk = load(2, wk_in, w.at[:, pl.ds(0, HD)])
    load_wv = load(3, wv_in, w.at[:, pl.ds(HD, HD)])
    load_q = load(4, q_in, qs)
    load_g = load(5, g_in, gs)
    load_gain.start()

    def norm_parts():
        hf = hbuf[...].astype(F32)
        inv = lax.rsqrt(jnp.mean(hf * hf, axis=1, keepdims=True) + EPS)
        return inv, hf * inv

    @pl.when(s == 7)
    def _():
        load_enc.start()

    @pl.when(is_dec)
    def _():
        load_wk.start()
        load_wv.start()
        load_q.start()
        load_g.start()

    load_gain.wait()

    @pl.when(s == 7)
    def _():
        load_enc.wait()
        _, normed = norm_parts()
        memory = (normed * gain[...]).astype(BF)
        for j in range(4):
            memsrc[j] = memory[:, j * 1024 : (j + 1) * 1024]

    pl.semaphore_wait(bar, 30 + lax.rem(2 * zl, 3) + zl // 3)

    def chunk(cc, hh, xx, jj):
        return mem.at[jj * 16 + cc * 8 + hh * 4 + xx]

    def piece(ref, f):
        return ref.at[pl.ds(f * ROWS, ROWS)]

    def rsem(hh, i, k, f):
        return rs.at[hh, i, k + 1, f]

    def spread(src, f):
        i = x + (y - x) * h
        for zz, hh in ((2, 0), (3, 0), (2, 1), (3, 1)):
            dev = (zz * 4 + y, dp_of(x, hh))
            copy(piece(src, f), piece(chunk(c, h, x, y), f), ssem.at[0], rsem(h, i, 0, f), dev).start()

    @pl.when(s == 7)
    def _():
        for f in range(PARTS):
            for j in (1, 0, 2):
                copy(piece(memsrc.at[j], f), piece(rbuf, f), ssem.at[0], src_s.at[f], (4 + j, d)).start()
            spread(memsrc.at[3], f)
        sent(mem.at[pl.ds(0, 7)], ssem.at[0])

    @pl.when(is_relay & (s != 7))
    def _():
        for f in range(PARTS):
            arrived(piece(rbuf, f), src_s.at[f])
            spread(rbuf, f)
        sent(mem.at[pl.ds(0, 4)], ssem.at[0])

    @pl.when(is_dec)
    def _():
        def send(src, dst, rsem, dev):
            copy(src, dst, ssem.at[0], rsem, dev).start()

        def at_y(k):
            return (zl * 4 + mod(y + k, 4), d)

        def at_x(k):
            return (s, dp_of(mod(x + k, 4), h))

        def pass_on(hh, xx, jj, f, to):
            ref = piece(chunk(c, hh, xx, jj), f)
            for dev, sem in to:
                send(ref, ref, sem, dev)
            send(ref, ref, rp.at[0], (s, partner))

        def got(hh, xx, jj, f, sem):
            arrived(piece(chunk(c, hh, xx, jj), f), sem)

        for f in range(PARTS):
            on_x = [(at_x(k), rsem(0, x, 0, f)) for k in (1, -1, 2)]
            on_y = [(at_y(k), rsem(1, y, 0, f)) for k in (1, -1, 2)]
            got(0, x, y, f, rsem(0, x, 0, f))
            pass_on(0, x, y, f, on_x + [(at_y(k), rsem(0, x, -k, f)) for k in (1, -1)])
            got(1, x, y, f, rsem(1, y, 0, f))
            pass_on(1, x, y, f, on_y + [(at_x(k), rsem(1, y, -k, f)) for k in (1, -1)])
        for f in range(PARTS):
            for k in (1, -1, 2):
                i, j = mod(x + k, 4), mod(y + k, 4)
                got(0, i, y, f, rsem(0, i, 0, f))
                pass_on(0, i, y, f, [(at_y(n), rsem(0, i, -n, f)) for n in (1, -1)])
                got(1, x, j, f, rsem(1, j, 0, f))
                pass_on(1, x, j, f, [(at_x(n), rsem(1, j, -n, f)) for n in (1, -1)])
        for f in range(PARTS):
            for k0 in (0, 1, -1, 2):
                i, j = mod(x + k0, 4), mod(y + k0, 4)
                for k in (-1, 1):
                    fwd = (k0 in (0, -1)) == (k == -1)
                    got(0, i, mod(y + k, 4), f, rsem(0, i, k, f))
                    pass_on(0, i, mod(y + k, 4), f, [(at_y(-k), far_s.at[0, f])] if fwd else [])
                    got(1, mod(x + k, 4), j, f, rsem(1, j, k, f))
                    pass_on(1, mod(x + k, 4), j, f, [(at_x(-k), far_s.at[1, f])] if fwd else [])
        for f in range(PARTS):
            arrived(mem.at[pl.ds(0, 4 // PARTS)], far_s.at[0, f])
            for k0 in (0, 1, -1, 2):
                pass_on(0, mod(x + k0, 4), mod(y + 2, 4), f, [])
            arrived(mem.at[pl.ds(0, 4 // PARTS)], far_s.at[1, f])
            for k0 in (0, 1, -1, 2):
                pass_on(1, mod(x + 2, 4), mod(y + k0, 4), f, [])

        load_wk.wait()
        load_wv.wait()

        def project(cc):
            acc[...] = jnp.zeros_like(acc)

            def step(j, _):
                rows = mem[pl.ds(j * 16 + cc * 8, 8)].reshape(256, 1024)
                wj = w[pl.ds(pl.multiple_of(j * 1024, 1024), 1024), :]
                acc[...] += jnp.dot(rows, wj, preferred_element_type=F32)
                return 0

            lax.fori_loop(0, 4, step, 0)
            kv[pl.ds(cc * 8, 8)] = acc[...].astype(BF).reshape(8, SRC, 512)

        def send_kv(t, group):
            copy(kv.at[p_of(t)], kvall.at[d], kvss.at[0], kvs.at[group], (s, t)).start()

        def other(k, cc):
            return 2 * lax.rem(d // 2 + k, 8) + cc

        project(c)
        for k in range(1, 8):
            send_kv(other(k, c), k // 4)
        kvall[d] = kv[my_p]
        arrived(mem.at[pl.ds(0, 32)], rp.at[0])
        save_mem = pltpu.make_async_copy(mem, mem_out, lsem.at[6])
        save_mem.start()
        project(1 - c)
        for k in range(8):
            send_kv(other(k, 1 - c), 2 + k // 4)
        sent(mem.at[pl.ds(0, 62)], ssem.at[0])
        load_q.wait()
        load_g.wait()
        valid = lax.broadcasted_iota(jnp.int32, (SRC, TGT), 0) < mlen[0]

        def head(a):
            cols = pl.ds(pl.multiple_of(a * HD, HD), HD)
            key = kvall[a, :, 0:HD]
            value = kvall[a, :, HD : 2 * HD]
            q = qs[:, cols]
            g = gs[:, cols]
            sc = lax.dot_general(key, q, NT, preferred_element_type=F32) * SCALE
            sc = jnp.where(valid, sc, -1e30)
            e = jnp.exp(sc - jnp.max(sc, axis=0, keepdims=True))
            pr = e / jnp.sum(e, axis=0, keepdims=True)
            gp = lax.dot_general(value, g, NT, preferred_element_type=F32)
            delta = jnp.sum(pr * gp, axis=0, keepdims=True)
            gsr = (pr * (gp - delta) * SCALE).astype(BF)
            kvg[a, :, 0:HD] = jnp.dot(gsr, q, preferred_element_type=F32).astype(BF)
            kvg[a, :, HD : 2 * HD] = jnp.dot(pr.astype(BF), g, preferred_element_type=F32).astype(BF)
            qgs[:, cols] = lax.dot_general(gsr, key, TN, preferred_element_type=F32).astype(BF)

        def send_back(a):
            copy(kvg.at[a], kvgall.at[my_p], gss.at[0], gsem.at[0], (s, a)).start()

        def heads(i, _):
            cc = c + i // 2 - 2 * c * (i // 2)
            ids = [2 * mod(d // 2 - lax.rem(i * 4 + n, 8), 8) + cc for n in range(4)]

            @pl.when(i == 0)
            def _():
                arrived(kvall.at[pl.ds(0, 3)], kvs.at[i])

            @pl.when(i != 0)
            def _():
                arrived(kvall.at[pl.ds(0, 4)], kvs.at[i])

            for a in ids:
                head(a)
            for a in ids:
                @pl.when(a != d)
                def _(a=a):
                    send_back(a)

            return 0

        lax.fori_loop(0, 4, heads, 0)
        kvgall[my_p] = kvg[d]
        save_qg = pltpu.make_async_copy(qgs, qg_out, lsem.at[7])
        save_qg.start()
        arrived(kvgall.at[pl.ds(0, 15)], gsem.at[0])
        save_kvg = pltpu.make_async_copy(kvgall, kvg_out, lsem.at[8])
        save_kvg.start()

        gacc[...] = jnp.zeros_like(gacc)
        order = [mod(y + k, 4) for k in (2, 1, -1, 0)]

        def grads(cc, j, put):
            def part(i, _):
                n0 = pl.multiple_of(i * 512, 512)
                left = kvgall[pl.ds(cc * 8, 8)].reshape(256, 512)
                wt = w[pl.ds(pl.multiple_of(j * 1024 + i * 512, 512), 512), :]
                tile = lax.dot_general(left, wt, NT, preferred_element_type=F32)
                m = mem[pl.ds(j * 16 + cc * 8, 8), :, pl.ds(n0, 512)].reshape(256, 512).astype(F32)
                gacc[j, :, pl.ds(n0, 512)] += jnp.sum((tile * m).reshape(32, 8, 512), axis=0)
                put(n0, tile.reshape(8, SRC, 512))
                return 0

            lax.fori_loop(0, 2, part, 0)

        def swap(j):
            return copy(dsend.at[j], drecv.at[j], dss.at[0], drs.at[j], (s, partner))

        def partner_rows(j):
            def put(n0, tile):
                dsend[j, :, :, pl.ds(n0, 512)] = tile.astype(BF)

            grads(1 - c, j, put)
            swap(j).start()

        def own_rows(j):
            swap(j).wait_recv()

            def put(n0, tile):
                cs[j, :, :, pl.ds(n0, 512)] = (tile + drecv[j, :, :, pl.ds(n0, 512)].astype(F32)).astype(BF)

            grads(c, j, put)

        def cut(hh, pos, i):
            return cs.at[pos, i] if hh == 0 else cs.at[i, 4 + pos]

        def along(hh, k):
            return at_y(k) if hh == 0 else at_x(k)

        def across(hh, k):
            return at_x(k) if hh == 0 else at_y(k)

        mine = (y, x)

        def far(hh, i):
            k = 1 - 2 * (i // 2)
            send(cut(hh, mod(mine[hh] + 2, 4), i), relay.at[hh, i], rel_s.at[hh, i // 2], along(hh, k))

        def near(hh, i, k):
            side = (1 - k) // 2
            send(cut(hh, mod(mine[hh] + k, 4), i), fin.at[hh, side, i], fin_s.at[hh], along(hh, k))

        for n in range(3):
            partner_rows(order[n])
        for n in range(4):
            own_rows(order[n])
            if n == 0:
                partner_rows(order[3])
                for i in range(4):
                    far(0, i)
            if n == 1:
                near(0, 2, 1)
                near(0, 3, 1)
            if n == 2:
                near(0, 0, -1)
                near(0, 1, -1)
            far(1, order[n])
        for i in range(4):
            near(1, i, -1 if i < 2 else 1)

        for t in range(16):
            part = gacc[t // 4, :, (t % 4) * 256 : (t % 4 + 1) * 256]
            g1[t] = jnp.sum(part, axis=0, keepdims=True)
        for k in range(1, 16):
            t = lax.rem(d + k, 16)
            copy(g1.at[t], g1r.at[d], g1ss.at[0], g1s.at[0], (s, t)).start()
        g1r[d] = g1[d]

        for half in range(2):
            for hh in range(2):
                k = 1 - 2 * half
                arrived(relay.at[hh, pl.ds(0, 2)], rel_s.at[hh, half])
                for i in (2 * half, 2 * half + 1):
                    ref = cut(hh, mod(mine[hh] + k, 4), i)
                    ref[...] = (ref[...].astype(F32) + relay[hh, i].astype(F32)).astype(BF)
                    near(hh, i, k)

        cross = (x, y)
        for hh in range(2):
            arrived(fin.at[hh], fin_s.at[hh])
            for i in range(4):
                rsum[hh, i] = (
                    cut(hh, mine[hh], i)[...].astype(F32) + fin[hh, 0, i].astype(F32) + fin[hh, 1, i].astype(F32)
                ).astype(BF)
            for k in (2, 1, 3):
                send(rsum.at[hh, mod(cross[hh] + k, 4)], peer.at[hh, k - 1], peer_s.at[hh], across(hh, k))
        arrived(g1r.at[pl.ds(0, 15)], g1s.at[0])
        g2[...] = jnp.sum(g1r[...], axis=0)
        for k in range(1, 16):
            copy(g2, g2r.at[s - 8], g2ss.at[0], g2s.at[0], (lax.rem(s + k, 16), d)).start()
        g2r[s - 8] = g2[...]

        for hh in range(2):
            total = rsum[hh, cross[hh]].astype(F32)
            arrived(peer.at[hh], peer_s.at[hh])
            for k in range(3):
                total = total + peer[hh, k].astype(F32)
            fchunk[hh] = total.astype(BF)
            slot = (zl - 2) * 2 + h
            send(fchunk.at[hh], zbuf.at[slot], z_s.at[0], (4 + y, dp_of(x, hh)))

    @pl.when(is_dec)
    def _():
        arrived(g2r.at[pl.ds(0, 7)], g2s.at[0])

    @pl.when(jnp.logical_not(is_dec))
    def _():
        arrived(g2r, g2s.at[0])

    g3r[d] = jnp.sum(g2r[...], axis=0) / gain[:, pl.ds(pl.multiple_of(d * 256, 256), 256)]
    for k in range(1, 16):
        copy(g3r.at[d], g3r.at[d], g3ss.at[0], g3s.at[0], (s, lax.rem(d + k, 16))).start()

    @pl.when(is_dec)
    def _():
        sent(mem.at[pl.ds(0, 32)], ssem.at[0])
        sent(kv.at[pl.ds(0, 15)], kvss.at[0])
        sent(kvg.at[pl.ds(0, 15)], gss.at[0])
        sent(dsend, dss.at[0])
        sent(g1.at[pl.ds(0, 15)], g1ss.at[0])
        sent(g1.at[pl.ds(0, 15)], g2ss.at[0])
        load(6, mem, mem_out).wait()
        load(7, qgs, qg_out).wait()
        load(8, kvgall, kvg_out).wait()

    @pl.when(is_relay)
    def _():
        total = jnp.zeros((SRC, 1024), F32)
        arrived(zbuf, z_s.at[0])
        for i in range(4):
            total = total + zbuf[i].astype(F32)
        ysum[...] = total.astype(BF)

    @pl.when(is_relay & (s != 7))
    def _():
        cp = copy(ysum, sbuf.at[y], ssem.at[0], y_s.at[0], (7, d))
        cp.start()
        cp.wait_send()

    @pl.when(s == 7)
    def _():
        inv, normed = norm_parts()
        arrived(sbuf.at[pl.ds(0, 3)], y_s.at[0])
        sbuf[3] = ysum[...]
        mgrad = jnp.concatenate([sbuf[j].astype(F32) for j in range(4)], axis=1)
        scaled = mgrad * gain[...]
        stv[...] = (inv * (scaled - normed * jnp.mean(scaled * normed, axis=1, keepdims=True))).astype(BF)

    @pl.when(s != 7)
    def _():
        stv[...] = jnp.zeros_like(stv)

    save_state = pltpu.make_async_copy(stv, state_out, lsem.at[6])
    save_state.start()
    arrived(g3r.at[pl.ds(0, 15)], g3s.at[0])
    save_gain = pltpu.make_async_copy(g3r, gain_out, lsem.at[7])
    save_gain.start()
    sent(g3r.at[pl.ds(0, 15)], g3ss.at[0])
    save_state.wait()
    save_gain.wait()


def exchange(enc, gain, q, g, wk, wv, mlen):
    any_spec = pl.BlockSpec(memory_space=pl.ANY)
    V = pltpu.VMEM
    S = pltpu.SemaphoreType.DMA
    return pl.pallas_call(
        body,
        name="relay_attention",
        out_shape=(
            jax.ShapeDtypeStruct((TGT, D), BF),
            jax.ShapeDtypeStruct((64, SRC, 1024), BF),
            jax.ShapeDtypeStruct((16, SRC, 512), BF),
            jax.ShapeDtypeStruct((SRC, D), BF),
            jax.ShapeDtypeStruct((16, 1, 256), F32),
        ),
        in_specs=[any_spec] * 6 + [pl.BlockSpec(memory_space=pltpu.SMEM)],
        out_specs=[any_spec] * 5,
        scratch_shapes=[
            V((SRC, D), BF),
            V((1, D), F32),
            V((4, SRC, 1024), BF),
            V((SRC, 1024), BF),
            V((64, SRC, 1024), BF),
            V((D, 512), BF),
            V((TGT, D), BF),
            V((TGT, D), BF),
            V((TGT, D), BF),
            V((256, 512), F32),
            V((16, SRC, 512), BF),
            V((16, SRC, 512), BF),
            V((16, SRC, 512), BF),
            V((16, SRC, 512), BF),
            V((4, 8, 1024), F32),
            V((4, 8, SRC, 1024), BF),
            V((4, 8, SRC, 1024), BF),
            V((4, 8, SRC, 1024), BF),
            V((2, 4, SRC, 1024), BF),
            V((2, 2, 4, SRC, 1024), BF),
            V((2, 4, SRC, 1024), BF),
            V((2, 3, SRC, 1024), BF),
            V((2, SRC, 1024), BF),
            V((4, SRC, 1024), BF),
            V((SRC, 1024), BF),
            V((4, SRC, 1024), BF),
            V((16, 1, 256), F32),
            V((16, 1, 256), F32),
            V((1, 256), F32),
            V((8, 1, 256), F32),
            V((16, 1, 256), F32),
            V((SRC, D), BF),
            S((9,)),
            S((1,)),
            S((PARTS,)),
            S((2, 4, 3, PARTS)),
            S((2, PARTS)),
            S((1,)),
            S((4,)),
            S((1,)),
            S((1,)),
            S((1,)),
            S((1,)),
            S((4,)),
            S((2, 2)),
            S((2,)),
            S((2,)),
            S((1,)),
            S((1,)),
            S((1,)),
            S((1,)),
            S((1,)),
            S((1,)),
            S((1,)),
            S((1,)),
        ],
        compiler_params=pltpu.CompilerParams(
            collective_id=0, has_side_effects=True, vmem_limit_bytes=60 * 1024 * 1024
        ),
    )(enc, gain, q, g, wk, wv, mlen)


def finish(
    qg_in, mem_in, kvg_in, state_in, gain_in,
    qg_out, kw_out, vw_out, state_out, gain_out,
    qg, mem, kvg, state, gain, kw, vw, ins, outs,
):
    is_dec = lax.axis_index("section") >= 8

    def into(i, src, dst):
        return pltpu.make_async_copy(src, dst, ins.at[i])

    def out(i, src, dst):
        return pltpu.make_async_copy(src, dst, outs.at[i])

    in_state, in_gain = into(0, state_in, state), into(1, gain_in, gain)
    out_state, out_gain = out(0, state, state_out), out(1, gain, gain_out)

    def store(j):
        rows = pl.ds(j * 1024, 1024)
        return out(2 + j, kw.at[rows], kw_out.at[rows]), out(6 + j, vw.at[rows], vw_out.at[rows])

    out_qg = out(10, qg, qg_out)

    @pl.when(is_dec)
    def _():
        in_kvg, in_qg = into(2, kvg_in, kvg), into(3, qg_in, qg)
        in_mem = [into(4 + j, mem_in.at[pl.ds(16 * j, 16)], mem.at[pl.ds(16 * j, 16)]) for j in range(4)]
        in_kvg.start()
        for cp in in_mem:
            cp.start()
        in_qg.start()
        in_state.start()
        in_gain.start()
        in_kvg.wait()
        for j in range(4):
            in_mem[j].wait()
            rows = mem[16 * j : 16 * (j + 1)].reshape(512, 1024)
            both = lax.dot_general(rows, kvg[...].reshape(512, 512), TN, preferred_element_type=F32).astype(BF)
            kw[j * 1024 : (j + 1) * 1024] = both[:, :HD]
            vw[j * 1024 : (j + 1) * 1024] = both[:, HD:]
            for cp in store(j):
                cp.start()
        in_qg.wait()
        out_qg.start()

    @pl.when(jnp.logical_not(is_dec))
    def _():
        in_state.start()
        in_gain.start()
        zero = kw.at[pl.ds(0, 1024)]
        zero[...] = jnp.zeros((1024, HD), BF)
        for j in range(4):
            rows = pl.ds(j * 1024, 1024)
            out(2 + j, zero, kw_out.at[rows]).start()
            out(6 + j, zero, vw_out.at[rows]).start()
        qg[...] = jnp.zeros_like(qg)
        out_qg.start()

    in_state.wait()
    out_state.start()
    in_gain.wait()
    out_gain.start()
    for j in range(4):
        for cp in store(j):
            cp.wait()
    for cp in (out_qg, out_state, out_gain):
        cp.wait()


def weight_grads(qg, mem, kvg, state, gain_grad):
    any_spec = pl.BlockSpec(memory_space=pl.ANY)
    V = pltpu.VMEM
    S = pltpu.SemaphoreType.DMA
    return pl.pallas_call(
        finish,
        name="weight_grads",
        out_shape=(
            jax.ShapeDtypeStruct((TGT, D), BF),
            jax.ShapeDtypeStruct((D, HD), BF),
            jax.ShapeDtypeStruct((D, HD), BF),
            jax.ShapeDtypeStruct((SRC, D), BF),
            jax.ShapeDtypeStruct((16, 1, 256), F32),
        ),
        in_specs=[any_spec] * 5,
        out_specs=[any_spec] * 5,
        scratch_shapes=[
            V((TGT, D), BF),
            V((64, SRC, 1024), BF),
            V((16, SRC, 512), BF),
            V((SRC, D), BF),
            V((16, 1, 256), F32),
            V((D, HD), BF),
            V((D, HD), BF),
            S((8,)),
            S((11,)),
        ],
        compiler_params=pltpu.CompilerParams(vmem_limit_bytes=60 * 1024 * 1024),
    )(qg, mem, kvg, state, gain_grad)


def on_device(enc_state, final_gain, queries, w_key, w_value, ctx_grad, mem_len):
    parts = exchange(
        enc_state[0], final_gain.reshape(1, D), queries[0], ctx_grad[0], w_key[0], w_value[0], mem_len
    )
    qg, kw, vw, state, gain_grad = weight_grads(*parts)
    return qg[None], kw[None], vw[None], state[None], gain_grad.reshape(D)


def solution(mesh):
    placed = (
        P("section", "dp", None),
        P(),
        P("section", "dp", None),
        P("section", None, "dp"),
        P("section", None, "dp"),
        P("section", "dp", None),
        P("dp"),
    )
    return jax.shard_map(
        on_device,
        mesh=mesh,
        in_specs=placed,
        out_specs=(
            P("section", "dp", None),
            P("section", None, "dp"),
            P("section", None, "dp"),
            P("section", "dp", None),
            P(),
        ),
        check_vma=False,
    )
```

time: 94.8 us -> 87.4 us (0.922)
  Pallas kernels: 93.4 us -> 85.9 us
    pallas_call x1, Pallas kernels: 87.5 us -> 80 us  [exchange(): pl.pallas_call(body, name='relay_attention', out_shape=(jax.ShapeDtypeStr...]
where the time goes in v3:
time: 87.4 us; the launch traced here: 87.2 us
  Pallas kernels  85.9 us (98%)
  between operations  1.29 us (1%)
    pallas_call x1, Pallas kernels, exchange(): pl.pallas_call(body, name='relay_attention', out_shape=(jax.ShapeDtypeStr...  80 us
    pallas_call x1, Pallas kernels, weight_grads(): pl.pallas_call(finish, name='weight_grads', out_shape=(jax.ShapeDtypeStru...  5.95 us

profile of v3, /device:TPU:65, one launch (start us, length us, event | category | flops | bytes accessed | tf_op | source)
XLA Modules:
  0.0 87.2 jit_solution(7881263091594223701)
XLA Ops:
  1.3 80.0 %relay_attention.1 = (bf16[128,4096]{1,0:T(8,128)(2,1)}, bf16[64,32,1024]{2,1,0:T(8,128)(2,1)}, bf16[16,32,512]{2,1,0:T(8,128)(2,1)}, bf16[32,4096]{1,0:T(8,128)(2,1)}, f32[16,1,256]{2,1,0:T(1,128)}) custom-call(bf16[32,4096]{1,0:T(8,128)(2,1)} %bitcast.15, f32[1,4096]{1,0:T(1,128)} %bitcast.16, bf16[128,4096]{1,0:T(8,128)(2,1)} %bitcast.13, ...), custom_call_target="tpu_custom_call" | custom-call | tf_op jit(solution)/shard_map/relay_attention/pallas_call | solution.py:463
  81.3 5.9 %weight_grads.1 = (bf16[128,4096]{1,0:T(8,128)(2,1)}, bf16[4096,256]{1,0:T(8,128)(2,1)}, bf16[4096,256]{1,0:T(8,128)(2,1)}, bf16[32,4096]{1,0:T(8,128)(2,1)}, f32[16,1,256]{2,1,0:T(1,128)}) custom-call(bf16[128,4096]{1,0:T(8,128)(2,1)} %get-tuple-element.15.qg_in, bf16[64,32,1024]{2,1,0:T(8,128)(2,1)} %get-tuple-element.16.mem_in, ...), custom_call_target="tpu_custom_call" | custom-call | tf_op jit(solution)/shard_map/weight_grads/pallas_call | solution.py:610
